TPU v7x, 128 devices: a whole 4x4x4 slice. The times are simulated.
128 devices in a mesh: section: 4 (over z), tile: 32 (over x, y, core).
Axes of the slice: x: 4, y: 4, z: 4, core: 2. Of those that a mesh axis runs over, the one named last changes fastest.
Arguments:
- surface: float32 [4, 4096, 16, 128], P('section', 'tile'), may hold values from -6 to 6
- surface_mask: int32 [4, 4096, 128], P('section', 'tile'), may hold values 0 or 1
- kappa: float32 [4, 16], P('section'), may hold values from 4 to 32
- remap_weights: bfloat16 [4, 4096, 4, 128, 128], P('section', 'tile'), may hold values from -0.25 to 0.25
- remap_columns: int32 [4, 4096, 4], P('section', 'tile'), may hold values from 0 to 16383, as said below
Outputs:
- new_surface: float32 [4, 4096, 16, 128], P('section', 'tile')
Inputs may be any that keep to these rules, and one draw needn't show every extreme that they name: `remap_columns`: for section 0 (atmosphere) every source block lies in sections 1 to 3; for sections 1 to 3 it lies in section 0. The source row lies in the destination row's tile of 128 rows or in one of the two tiles beside it.
All inputs are finite; a program needn't handle non-finite values. No bound on the sum of `surface_mask` on one device may be relied on, other than what follows from the above.
Results may differ from a plain program's by a relative error of at most 0.0011.
Values may be sent and summed in bfloat16 or wider, within the bound.
A program may use at most 128 MiB of HBM per device.

v0:
```python
import jax
import jax.numpy as jnp
from jax import lax
from jax.sharding import PartitionSpec as P

SWEEPS = 4


time_step = 0.5
zonal_ratio = 0.25


def joined_along(pieces, dim):
    pieces = jnp.moveaxis(pieces, 0, dim)
    dims = pieces.shape
    return pieces.reshape(*dims[:dim], dims[dim] * dims[dim + 1], *dims[dim + 2 :])


def sent_to_all(value, axis):
    copies = jnp.broadcast_to(value, (lax.axis_size(axis), *value.shape))
    return lax.all_to_all(copies, axis, split_axis=0, concat_axis=0, tiled=True)


def collect(value, axis, dim):
    return joined_along(sent_to_all(value, axis), dim)


def extended_2(block, sides, width):
    for axis, dim in sides:
        count = lax.axis_size(axis)
        forward = [(i, i + 1) for i in range(count - 1)]
        backward = [(target, source) for source, target in forward]
        low = lax.ppermute(
            lax.slice_in_dim(block, block.shape[dim] - width, None, axis=dim), axis, forward
        )
        high = lax.ppermute(lax.slice_in_dim(block, 0, width, axis=dim), axis, backward)
        block = jnp.concatenate([low, block, high], axis=dim)
    return block


def jacobi_update(padded, current, right_side, meridional, zonal_coef, denominator):
    vertical = padded[:-2] + padded[2:]
    zonal_sum = jnp.roll(current, 1, 2) + jnp.roll(current, -1, 2)
    return (right_side + meridional * vertical + zonal_coef * zonal_sum) / denominator


def body(surface, surface_mask, kappa, remap_weights, remap_columns):
    rows_dev = surface.shape[1]
    tile_count = lax.axis_size("tile")
    tile_index = lax.axis_index("tile")
    total_rows = rows_dev * tile_count
    sent_fields = surface[0].astype(jnp.bfloat16)
    stacked = collect(sent_fields[None], "section", 0)
    window = extended_2(stacked, (("tile", 1),), rows_dev)
    candidates = window.reshape((window.shape[0] * window.shape[1],) + window.shape[2:])
    columns = remap_columns[0]
    section_of = columns // total_rows
    row_of = columns - section_of * total_rows
    local_index = section_of * (3 * rows_dev) + row_of - (tile_index - 1) * rows_dev
    picked = jnp.take(candidates, local_index.reshape(-1), axis=0)
    picked = picked.reshape(columns.shape + candidates.shape[1:])
    forcing = jnp.einsum(
        "rkij,rkfj->rfi", remap_weights[0], picked, preferred_element_type=jnp.float32
    )
    mask_values = surface_mask[0].astype(jnp.float32)[:, None, :]
    right_side = surface[0] + time_step * mask_values * forcing
    meridional = kappa[0][None, :, None]
    zonal_coef = zonal_ratio * meridional
    denominator = 1.0 + 2.0 * meridional + 2.0 * zonal_coef
    extended = extended_2(right_side, (("tile", 0),), SWEEPS)
    global_row = tile_index * rows_dev - SWEEPS + jnp.arange(rows_dev + 2 * SWEEPS, dtype=jnp.int32)
    inside = ((global_row >= 0) & (global_row < total_rows))[:, None, None]
    iterate = extended
    for sweep_index in range(SWEEPS):
        padded = jnp.pad(iterate, ((1, 1), (0, 0), (0, 0)))
        updated = jacobi_update(padded, iterate, extended, meridional, zonal_coef, denominator)
        iterate = jnp.where(inside, updated, 0.0)
    iterate = iterate[SWEEPS : SWEEPS + rows_dev]
    return iterate[None]


def solution(mesh):
    return jax.shard_map(
        body,
        mesh=mesh,
        in_specs=(
            P("section", "tile", None, None),
            P("section", "tile", None),
            P("section", None),
            P("section", "tile", None, None, None),
            P("section", "tile", None),
        ),
        out_specs=P("section", "tile", None, None),
        check_vma=False,
    )
```

profile of v0, /device:TPU:6, one launch (start us, length us, event | category | flops | bytes accessed | tf_op | source)
XLA Modules:
  0.0 100.0 jit_solution(17282455987035130466)
XLA Ops:
  0.0 1.3 %bitcast_convert_fusion = bf16[128,16,128]{2,1,0:T(8,128)(2,1)S(1)} fusion(f32[1,128,16,128]{3,2,1,0:T(8,128)} %param.5), kind=kLoop, calls=%fused_computation.38 | loop fusion | flops 262144 | bytes 1572864 | tf_op jit(solution)/shard_map/convert_element_type | solution.py:52
  1.3 0.3 broadcast_in_dim.45
  1.6 0.0 copy-start.2
  1.6 31.6 %all_to_all.5 = bf16[4,1,128,16,128]{4,3,2,1,0:T(8,128)(2,1)S(1)} all-to-all(bf16[4,1,128,16,128]{4,3,2,1,0:T(8,128)(2,1)S(1)} %broadcast_in_dim.45), channel_id=1, replica_groups=mesh['section'=4,'tile'=32] {'section'}, dimensions={0} | all-to-all | bytes 4194304 | tf_op jit(solution)/shard_map/all_to_all | solution.py:21
  33.2 1.9 %collective-permute-start = (bf16[4,128,16,128]{3,2,1,0:T(8,128)(2,1)S(1)}, bf16[4,128,16,128]{3,2,1,0:T(8,128)(2,1)}, u32[]{:S(2)}, u32[]{:S(2)}) collective-permute-start(bf16[4,128,16,128]{3,2,1,0:T(8,128)(2,1)S(1)} %bitcast.57), channel_id=1, source_target_pairs={{0,1},{1,2},{2,3},{3,4},{4,5},{5,6},{6,7},{7,8},{8,9},{9,10},{10,1... | collective-permute-start | bytes 6291464 | tf_op jit(solution)/shard_map/ppermute | solution.py:33
  35.1 5.8 %collective-permute-start.1 = (bf16[4,128,16,128]{3,2,1,0:T(8,128)(2,1)S(1)}, bf16[4,128,16,128]{3,2,1,0:T(8,128)(2,1)}, u32[]{:S(2)}, u32[]{:S(2)}) collective-permute-start(bf16[4,128,16,128]{3,2,1,0:T(8,128)(2,1)S(1)} %bitcast.58), channel_id=1, source_target_pairs={{1,0},{2,1},{3,2},{4,3},{5,4},{6,5},{7,6},{8,7},{9,8},{10,9},{11,1... | collective-permute-start | bytes 6291464 | tf_op jit(solution)/shard_map/ppermute | solution.py:36
  40.9 0.1 copy.8
  41.0 0.1 squeeze.15
  41.1 0.1 copy.7
  41.4 21.4 %collective-permute-done = bf16[4,128,16,128]{3,2,1,0:T(8,128)(2,1)} collective-permute-done((bf16[4,128,16,128]{3,2,1,0:T(8,128)(2,1)S(1)}, bf16[4,128,16,128]{3,2,1,0:T(8,128)(2,1)}, u32[]{:S(2)}, u32[]{:S(2)}) %collective-permute-start) | collective-permute-done | bytes 2097184 | tf_op jit(solution)/shard_map/ppermute | solution.py:33
  62.7 1.7 %collective-permute-done.1 = bf16[4,128,16,128]{3,2,1,0:T(8,128)(2,1)} collective-permute-done((bf16[4,128,16,128]{3,2,1,0:T(8,128)(2,1)S(1)}, bf16[4,128,16,128]{3,2,1,0:T(8,128)(2,1)}, u32[]{:S(2)}, u32[]{:S(2)}) %collective-permute-start.1) | collective-permute-done | bytes 2097184 | tf_op jit(solution)/shard_map/ppermute | solution.py:36
  64.4 5.5 %pad_maximum_fusion = bf16[4,384,16,128]{3,2,1,0:T(8,128)(2,1)} fusion(bf16[4,128,16,128]{3,2,1,0:T(8,128)(2,1)} %collective-permute-done.1, bf16[4,128,16,128]{3,2,1,0:T(8,128)(2,1)S(1)} %bitcast.59, bf16[4,128,16,128]{3,2,1,0:T(8,128)(2,1)} %collective-permute-done), kind=kLoop, calls=%fused_computation.3 | loop fusion | flops 6291456 | bytes 12582912 | tf_op jit(solution)/shard_map/concatenate | solution.py:37
  69.9 4.1 %gather_fusion = bf16[512,16,128]{2,1,0:T(8,128)(2,1)S(1)} fusion(bf16[1536,16,128]{2,1,0:T(8,128)(2,1)} %bitcast.55, s32[1024]{0:T(1024)S(1)} %pad_clamp_fusion), kind=kCustom, calls=%fused_computation | custom fusion | bytes 4196352 | tf_op jit(solution)/shard_map/jit(_take)/gather | solution.py:60
  74.0 8.1 %fusion.14 = f32[128,16,128]{2,1,0:T(8,128)S(1)} fusion(bf16[1,128,4,128,128]{4,3,2,1,0:T(8,128)(2,1)} %param.8, bf16[128,4,16,128]{3,2,1,0:T(8,128)(2,1)S(1)} %bitcast.56, pred[128,4]{1,0:T(8,128)(4,1)S(1)} %copy.7, f32[1,128,16,128]{3,2,1,0:T(8,128)S(1)} %copy-done, f32[128,128]{1,0:T(8,128)S(1)} %multiply_bitcast_fusion), kind=kOutput, calls=%fused_computation.8 | convolution fusion | flops 270008320 | bytes 21037568 | tf_op jit(solution)/shard_map/rkij,rkfj->rfi/dot_general | solution.py:62
  82.1 1.9 %collective-permute-start.2 = (f32[4,16,128]{2,1,0:T(8,128)S(1)}, f32[4,16,128]{2,1,0:T(8,128)S(1)}, u32[]{:S(2)}, u32[]{:S(2)}) collective-permute-start(f32[4,16,128]{2,1,0:T(8,128)S(1)} %get-tuple-element.23), channel_id=1, source_target_pairs={{0,1},{1,2},{2,3},{3,4},{4,5},{5,6},{6,7},{7,8},{8,9},{9,10},{10,1... | collective-permute-start | bytes 98312 | tf_op jit(solution)/shard_map/ppermute | solution.py:33
  84.0 6.0 %collective-permute-start.3 = (f32[4,16,128]{2,1,0:T(8,128)S(1)}, f32[4,16,128]{2,1,0:T(8,128)S(1)}, u32[]{:S(2)}, u32[]{:S(2)}) collective-permute-start(f32[4,16,128]{2,1,0:T(8,128)S(1)} %get-tuple-element.24), channel_id=1, source_target_pairs={{1,0},{2,1},{3,2},{4,3},{5,4},{6,5},{7,6},{8,7},{9,8},{10,9},{11,1... | collective-permute-start | bytes 98312 | tf_op jit(solution)/shard_map/ppermute | solution.py:36
  90.1 0.1 slice.135
  90.1 1.5 %collective-permute-done.3 = f32[4,16,128]{2,1,0:T(8,128)S(1)} collective-permute-done((f32[4,16,128]{2,1,0:T(8,128)S(1)}, f32[4,16,128]{2,1,0:T(8,128)S(1)}, u32[]{:S(2)}, u32[]{:S(2)}) %collective-permute-start.3) | collective-permute-done | bytes 32800 | tf_op jit(solution)/shard_map/ppermute | solution.py:36
  91.6 0.1 pad_maximum_fusion.1
  91.7 0.4 fusion.51
  92.1 0.4 fusion.52
  92.4 0.9 fusion.22
  93.3 0.4 fusion.49
  93.7 0.4 fusion.50
  94.0 1.3 %fusion.26 = f32[136,16,128]{2,1,0:T(8,128)S(1)} fusion(f32[136,16,127]{2,1,0:T(8,128)S(1)} %get-tuple-element.16, f32[136,16,1]{2,1,0:T(8,128)S(1)} %get-tuple-element.18, f32[136,16,1]{2,1,0:T(8,128)S(1)} %get-tuple-element.17, f32[136,16,127]{2,1,0:T(8,128)S(1)} %get-tuple-element.15, f32[136,16,128]{2,1,0:T(8,128)S(1)} %fusion.22, ...), kind=kLoop, calls=%fused_computation.19 | loop fusion | flops 3342336 | bytes 5570888 | tf_op jit(solution)/shard_map/jit(_where)/select_n | solution.py:77
  95.3 0.4 fusion.47
  95.7 0.4 fusion.48
  96.0 1.3 %fusion.30 = f32[136,16,128]{2,1,0:T(8,128)S(1)} fusion(f32[136,16,127]{2,1,0:T(8,128)S(1)} %get-tuple-element.12, f32[136,16,1]{2,1,0:T(8,128)S(1)} %get-tuple-element.14, f32[136,16,1]{2,1,0:T(8,128)S(1)} %get-tuple-element.13, f32[136,16,127]{2,1,0:T(8,128)S(1)} %get-tuple-element.11, f32[136,16,128]{2,1,0:T(8,128)S(1)} %fusion.26, ...), kind=kLoop, calls=%fused_computation.24 | loop fusion | flops 3342336 | bytes 5570888 | tf_op jit(solution)/shard_map/jit(_where)/select_n | solution.py:77
  97.4 0.4 fusion.46
  97.7 0.1 pad_slice_fusion.1
  97.9 0.4 fusion.45
  98.3 1.7 %fusion.34 = f32[1,128,16,128]{3,2,1,0:T(8,128)} fusion(f32[136,16,128]{2,1,0:T(8,128)S(1)} %pad_maximum_fusion.1, f32[136,16,127]{2,1,0:T(8,128)S(1)} %get-tuple-element.8, f32[136,16,1]{2,1,0:T(8,128)S(1)} %get-tuple-element.10, f32[136,16,1]{2,1,0:T(8,128)S(1)} %get-tuple-element.9, f32[136,16,127]{2,1,0:T(8,128)S(1)} %get-tuple-element.7, ...), kind=kLoop, calls=%fused_computation.31 | loop fusion | flops 2621440 | bytes 6422848 | tf_op jit(solution)/shard_map/broadcast_in_dim | solution.py:79
  (15 shorter events, 0.1 us)
Async XLA Ops:
  1.6 39.3 %copy-start.3 = (s32[1,128,4]{1,2,0:T(4,128)S(1)}, s32[1,128,4]{1,2,0:T(4,128)}, u32[]{:S(2)}) copy-start(s32[1,128,4]{1,2,0:T(4,128)} %param.9) | copy-start | bytes 6148
  1.6 39.7 %copy-start.2 = (f32[1,16]{1,0:T(1,128)S(1)}, f32[1,16]{1,0:T(1,128)}, u32[]{:S(2)}) copy-start(f32[1,16]{1,0:T(1,128)} %param.7) | copy-start | bytes 196
  1.6 39.7 %copy-start.1 = (s32[1,128,128]{2,1,0:T(8,128)S(1)}, s32[1,128,128]{2,1,0:T(8,128)}, u32[]{:S(2)}) copy-start(s32[1,128,128]{2,1,0:T(8,128)} %param.6) | copy-start | bytes 196612
  33.2 29.6 %collective-permute-start = (bf16[4,128,16,128]{3,2,1,0:T(8,128)(2,1)S(1)}, bf16[4,128,16,128]{3,2,1,0:T(8,128)(2,1)}, u32[]{:S(2)}, u32[]{:S(2)}) collective-permute-start(bf16[4,128,16,128]{3,2,1,0:T(8,128)(2,1)S(1)} %bitcast.57), channel_id=1, source_target_pairs={{0,1},{1,2},{2,3},{3,4},{4,5},{5,6},{6,7},{7,8},{8,9},{9,10},{10,1... | collective-permute-start | bytes 6291464 | tf_op jit(solution)/shard_map/ppermute | solution.py:33
  35.1 29.3 %collective-permute-start.1 = (bf16[4,128,16,128]{3,2,1,0:T(8,128)(2,1)S(1)}, bf16[4,128,16,128]{3,2,1,0:T(8,128)(2,1)}, u32[]{:S(2)}, u32[]{:S(2)}) collective-permute-start(bf16[4,128,16,128]{3,2,1,0:T(8,128)(2,1)S(1)} %bitcast.58), channel_id=1, source_target_pairs={{1,0},{2,1},{3,2},{4,3},{5,4},{6,5},{7,6},{8,7},{9,8},{10,9},{11,1... | collective-permute-start | bytes 6291464 | tf_op jit(solution)/shard_map/ppermute | solution.py:36
  69.9 4.1 %copy-start = (f32[1,128,16,128]{3,2,1,0:T(8,128)S(1)}, f32[1,128,16,128]{3,2,1,0:T(8,128)}, u32[]{:S(2)}) copy-start(f32[1,128,16,128]{3,2,1,0:T(8,128)} %param.5) | copy-start | bytes 3145732
  82.1 8.1 %collective-permute-start.2 = (f32[4,16,128]{2,1,0:T(8,128)S(1)}, f32[4,16,128]{2,1,0:T(8,128)S(1)}, u32[]{:S(2)}, u32[]{:S(2)}) collective-permute-start(f32[4,16,128]{2,1,0:T(8,128)S(1)} %get-tuple-element.23), channel_id=1, source_target_pairs={{0,1},{1,2},{2,3},{3,4},{4,5},{5,6},{6,7},{7,8},{8,9},{9,10},{10,1... | collective-permute-start | bytes 98312 | tf_op jit(solution)/shard_map/ppermute | solution.py:33
  84.0 7.6 %collective-permute-start.3 = (f32[4,16,128]{2,1,0:T(8,128)S(1)}, f32[4,16,128]{2,1,0:T(8,128)S(1)}, u32[]{:S(2)}, u32[]{:S(2)}) collective-permute-start(f32[4,16,128]{2,1,0:T(8,128)S(1)} %get-tuple-element.24), channel_id=1, source_target_pairs={{1,0},{2,1},{3,2},{4,3},{5,4},{6,5},{7,6},{8,7},{9,8},{10,9},{11,1... | collective-permute-start | bytes 98312 | tf_op jit(solution)/shard_map/ppermute | solution.py:36
where the time goes:
time: 102 us; the launch traced here: 100 us
  blocking collectives  31.6 us (31%)
  waiting for transfers between devices  24.5 us (24%)
  starting transfers between devices  15.6 us (15%)
  other arithmetic  12.1 us (12%)
  matrix products  8.11 us (8%)
  local copies, waits for them, and re-layouts  7.86 us (8%)
    all_to_all x1, blocking collectives, sent_to_all(): return lax.all_to_all(copies, axis, split_axis=0, concat_axis=0, tiled=True)  31.6 us
    ppermute x2, waiting for transfers between devices, extended_2(): lax.ppermute(lax.slice_in_dim(block, block.shape[dim] - width, None, axis...  21.4 us
    ppermute x2, starting transfers between devices, extended_2(): lax.ppermute(lax.slice_in_dim(block, 0, width, axis=dim), axis, backward)  11.8 us
    dot_general x1, matrix products, body(): jnp.einsum('rkij,rkfj->rfi', remap_weights[0], picked, preferred_element_...  8.11 us
    concatenate x2, other arithmetic, extended_2(): block = jnp.concatenate([low, block, high], axis=dim)  5.55 us
    gather x1, local copies, waits for them, and re-layouts, body(): picked = jnp.take(candidates, local_index.reshape(-1), axis=0)  4.06 us
    ppermute x2, starting transfers between devices, extended_2(): lax.ppermute(lax.slice_in_dim(block, block.shape[dim] - width, None, axis...  3.83 us
    select_n x3, other arithmetic, body(): iterate = jnp.where(inside, updated, 0.0)  3.45 us
  transfers between devices with their start and end apart: 4, of which 3 were waited for; matrix products, arithmetic and copies ran while one was open for 1% of the time, Pallas kernels for 0%

commit v1 on v0

v1 whole, which is shorter than its diff:
```python
import functools

import jax
import jax.numpy as jnp
from jax import lax
from jax.experimental import pallas as pl
from jax.experimental.pallas import tpu as pltpu
from jax.sharding import PartitionSpec as P

SWEEPS = 4
TIME_STEP = 0.5
ZONAL_RATIO = 0.25

CHUNK = 16
GROUP = 28
WPIECES = 16

NT = (((1,), (1,)), ((), ()))
F32 = jnp.float32


def remote(src, dst, send_sem, recv_sem, where):
    return pltpu.make_async_remote_copy(
        src_ref=src, dst_ref=dst, send_sem=send_sem, recv_sem=recv_sem,
        device_id=where, device_id_type=pl.DeviceIdType.MESH,
    )


def kernel(
    tiles, surf_hbm, mask_hbm, kappa_hbm, w_hbm, cols_hbm, out,
    surf, mask, kappa, w, cols, sent, win, relay, edge, near, halo,
    surf_sem, w_sem, in_sem,
    z_send, z_recv, up_send, down_send, low_recv, high_recv, relay_recv, halo_send, halo_recv,
):
    rows, fields, cells = surf.shape
    blocks = w.shape[1]
    chunks = rows // CHUNK
    half = chunks // 2
    total = rows * tiles
    s = lax.axis_index("section")
    t = lax.axis_index("tile")
    s_up, s_down = lax.rem(s + 1, 4), lax.rem(s + 3, 4)
    has_low, has_high = t > 0, t < tiles - 1

    surf_in = [
        pltpu.make_async_copy(
            surf_hbm.at[0, pl.ds(p * (rows // 4), rows // 4)], surf.at[pl.ds(p * (rows // 4), rows // 4)], surf_sem.at[p]
        )
        for p in range(4)
    ]
    for copy in surf_in:
        copy.start()
    small_in = [
        pltpu.make_async_copy(cols_hbm, cols, in_sem.at[0]),
        pltpu.make_async_copy(mask_hbm.at[0], mask, in_sem.at[1]),
        pltpu.make_async_copy(kappa_hbm, kappa, in_sem.at[2]),
    ]
    for copy in small_in:
        copy.start()
    piece = rows // WPIECES
    w_in = [
        pltpu.make_async_copy(w_hbm.at[0, pl.ds(p * piece, piece)], w.at[pl.ds(p * piece, piece)], w_sem.at[p])
        for p in range(WPIECES)
    ]
    for copy in w_in:
        copy.start()

    barrier = pltpu.get_barrier_semaphore()
    for where in ({"section": s_up}, {"section": s_down}):
        pl.semaphore_signal(barrier, inc=1, device_id=where, device_id_type=pl.DeviceIdType.MESH)

    @pl.when(has_low)
    def _():
        pl.semaphore_signal(barrier, inc=1, device_id={"tile": t - 1}, device_id_type=pl.DeviceIdType.MESH)

    @pl.when(has_high)
    def _():
        pl.semaphore_signal(barrier, inc=1, device_id={"tile": t + 1}, device_id_type=pl.DeviceIdType.MESH)

    for p in range(4):
        surf_in[p].wait()
        part = pl.ds(p * (rows // 4), rows // 4)
        sent[part] = surf[part].astype(jnp.bfloat16)

    pl.semaphore_wait(barrier, 2 + has_low.astype(jnp.int32) + has_high.astype(jnp.int32))

    def at(start, q):
        return win.at[pl.ds(start + q * CHUNK, CHUNK)]

    def mine(q):
        return sent.at[pl.ds(q * CHUNK, CHUNK)]

    def to_low(base, q, n):
        return remote(at(base + rows, q), at(base + 2 * rows, q), down_send.at[n], high_recv.at[n], {"tile": t - 1})

    def to_high(base, q, n):
        return remote(at(base + rows, q), at(base, q), up_send.at[n], low_recv.at[n], {"tile": t + 1})

    def spread(base, q, n):
        @pl.when(has_low)
        def _():
            to_low(base, q, n).start()

        @pl.when(has_high)
        def _():
            to_high(base, q, n).start()

    def arrived(base, q, n):
        remote(mine(q), at(base + rows, q), z_send.at[n], z_recv.at[n], {"section": s_up}).wait_recv()

    def finish(count):
        def step(n, _):
            base, q = (n // chunks) * (3 * rows), lax.rem(n, chunks)

            @pl.when(has_low)
            def _():
                to_high(base, q, n).wait_recv()

            @pl.when(has_high)
            def _():
                to_low(base, q, n).wait_recv()

            return 0

        lax.fori_loop(0, count, step, 0)

    def finish_sends(count):
        def step(n, _):
            base, q = (n // chunks) * (3 * rows), lax.rem(n, chunks)

            @pl.when(has_low)
            def _():
                to_low(base, q, n).wait_send()

            @pl.when(has_high)
            def _():
                to_high(base, q, n).wait_send()

            return 0

        lax.fori_loop(0, count, step, 0)

    @pl.when(s == 0)
    def _():
        for q in range(chunks):
            remote(mine(q), at(rows, q), z_send.at[q], z_recv.at[q], {"section": s_up}).start()
            other = (q + half) % chunks
            remote(mine(other), at(rows, other), z_send.at[chunks + other], z_recv.at[other], {"section": s_down}).start()

        def direct(q, _):
            for src in (0, 2):
                n = src * chunks + q
                arrived(src * 3 * rows, q, n)
                spread(src * 3 * rows, q, n)
            return 0

        lax.fori_loop(0, chunks, direct, 0)

        def relayed(q, _):
            for h in range(2):
                n = chunks + h * half + q
                arrived(3 * rows, h * half + q, n)
                spread(3 * rows, h * half + q, n)
            return 0

        lax.fori_loop(0, half, relayed, 0)
        finish(3 * chunks)

    @pl.when((s == 1) | (s == 3))
    def _():
        h = s // 2
        base = (s - 1) * (3 * rows)
        far = 2
        for q in range(chunks):
            remote(mine(q), at(base + rows, q), z_send.at[q], z_recv.at[(s - 1) * chunks + q], {"section": 0}).start()

        def step(q, _):
            own = h * half + q
            held = relay.at[pl.ds(q * CHUNK, CHUNK)]
            arrived(0, own, own)
            remote(at(rows, own), at(rows, own), z_send.at[chunks + half + q], z_recv.at[own], {"section": far}).start()
            spread(0, own, own)
            remote(mine(q), held, z_send.at[q], relay_recv.at[q], {"section": far}).wait_recv()
            remote(
                held, at(4 * rows, own), z_send.at[chunks + q], z_recv.at[chunks + own], {"section": 0}
            ).start()
            return 0

        lax.fori_loop(0, half, step, 0)

        def rest(q, _):
            other = (1 - h) * half + q
            arrived(0, other, other)
            spread(0, other, other)
            return 0

        lax.fori_loop(0, half, rest, 0)
        finish(chunks)

    @pl.when(s == 2)
    def _():
        for q in range(half):
            held = relay.at[pl.ds(q * CHUNK, CHUNK)]
            remote(mine(q), held, z_send.at[q], relay_recv.at[q], {"section": 1}).start()
            remote(mine(half + q), held, z_send.at[half + q], relay_recv.at[q], {"section": 3}).start()

        def step(q, _):
            for n in (q, half + q):
                arrived(0, n, n)
                spread(0, n, n)
            return 0

        lax.fori_loop(0, half, step, 0)
        finish(chunks)

    for copy in small_in:
        copy.wait()
    for copy in w_in:
        copy.wait()

    offset = (1 - t) * rows - jnp.where(s == 0, 3 * rows, 0)
    lane = lax.broadcasted_iota(jnp.int32, (fields, fields), 1)
    sub = lax.broadcasted_iota(jnp.int32, (fields, fields), 0)
    diag = jnp.where(lane == sub, jnp.broadcast_to(kappa[0:1, :], (fields, fields)), 0.0)
    kap = jnp.broadcast_to(jnp.sum(diag, axis=1, keepdims=True), (fields, cells))
    inv = 1.0 / (1.0 + 2.0 * kap + 2.0 * (ZONAL_RATIO * kap))
    a = kap * inv
    b = ZONAL_RATIO * kap * inv

    def forced(r):
        picks, weights = [], []
        for k in range(blocks):
            c = cols[k, r]
            place = c - (c // total) * (total - 3 * rows) + offset
            picks.append(win[jnp.clip(place, 0, 9 * rows - 1)])
            weights.append(w[r, k])
        forcing = lax.dot_general(
            jnp.concatenate(picks, axis=1), jnp.concatenate(weights, axis=1), NT, preferred_element_type=F32
        )
        scale = TIME_STEP * mask[pl.ds(r, 1), :].astype(F32)
        return surf[r] + scale * forcing

    def swept(base, low, mid, high):
        zonal = pltpu.roll(mid, 1, 1) + pltpu.roll(mid, cells - 1, 1)
        return base + a * (low + high) + b * zonal

    def advance(state, row):
        levels, bases = state
        levels, bases = [list(x) for x in levels], list(bases)
        bases.append(row * inv)
        levels[0].append(row)
        new = None
        for n in range(SWEEPS):
            if len(levels[n]) < 3:
                return (levels, bases), None
            new = swept(bases[-2 - n], *levels[n][-3:])
            levels[n] = levels[n][-2:]
            if n + 1 < SWEEPS:
                levels[n + 1].append(new)
        return (levels, bases[-SWEEPS - 1:]), new

    low_rows = [forced(r) for r in range(SWEEPS)]
    high_rows = [forced(rows - SWEEPS + r) for r in range(SWEEPS)]
    for r in range(SWEEPS):
        edge[0, r] = low_rows[r]
        edge[1, r] = high_rows[r]
    halo_low = remote(edge.at[0], halo.at[1], halo_send.at[0], halo_recv.at[1], {"tile": t - 1})
    halo_high = remote(edge.at[1], halo.at[0], halo_send.at[1], halo_recv.at[0], {"tile": t + 1})
    pl.when(has_low)(halo_low.start)
    pl.when(has_high)(halo_high.start)

    state = ([[] for _ in range(SWEEPS)], [])
    for r in range(2 * SWEEPS):
        if r < SWEEPS:
            row = low_rows[r]
        else:
            row = forced(r)
            near[0, r - SWEEPS] = row
        state, done = advance(state, row)
        if done is not None:
            out[0, r - SWEEPS] = done

    def pack(state):
        levels, bases = state
        return tuple(x for level in levels for x in level) + tuple(bases[-SWEEPS:])

    def unpack(flat):
        return [list(flat[2 * n : 2 * n + 2]) for n in range(SWEEPS)], list(flat[2 * SWEEPS :])

    first = 2 * SWEEPS
    count = (rows - 2 * SWEEPS - first) // GROUP

    def group(g, flat):
        state = unpack(flat)
        for u in range(GROUP):
            r = first + g * GROUP + u
            state, done = advance(state, forced(r))
            out[0, r - SWEEPS] = done
        return pack(state)

    state = unpack(lax.fori_loop(0, count, group, pack(state)))
    for r in range(first + count * GROUP, rows):
        if r < rows - SWEEPS:
            row = forced(r)
            if r >= rows - 2 * SWEEPS:
                near[1, r - (rows - 2 * SWEEPS)] = row
        else:
            row = edge[1, r - (rows - SWEEPS)]
        state, done = advance(state, row)
        out[0, r - SWEEPS] = done

    pl.when(has_low)(halo_high.wait_recv)
    pl.when(has_high)(halo_low.wait_recv)

    def end_rows(values, outside, lost):
        values = [jnp.where(lost, 0.0, v) if outside(i) else v for i, v in enumerate(values)]
        bases = [v * inv for v in values]
        level = values
        for n in range(SWEEPS):
            level = [
                jnp.where(lost, 0.0, v) if outside(n + 1 + i) else v
                for i, v in enumerate(
                    swept(bases[n + i], *level[i - 1 : i + 2]) for i in range(1, len(level) - 1)
                )
            ]
        return level

    low_values = [halo[0, r] for r in range(SWEEPS)] + [edge[0, r] for r in range(SWEEPS)]
    low_values += [near[0, r] for r in range(SWEEPS)]
    for r, v in enumerate(end_rows(low_values, lambda i: i < SWEEPS, jnp.logical_not(has_low))):
        out[0, r] = v
    high_values = [near[1, r] for r in range(SWEEPS)] + [edge[1, r] for r in range(SWEEPS)]
    high_values += [halo[1, r] for r in range(SWEEPS)]
    for r, v in enumerate(end_rows(high_values, lambda i: i >= 2 * SWEEPS, jnp.logical_not(has_high))):
        out[0, rows - SWEEPS + r] = v

    pl.when(has_low)(halo_low.wait_send)
    pl.when(has_high)(halo_high.wait_send)

    def sent_out(count):
        def step(n, _):
            remote(mine(0), at(rows, 0), z_send.at[n], z_recv.at[0], {"section": s_up}).wait_send()
            return 0

        lax.fori_loop(0, count, step, 0)

    sent_out(jnp.where(s == 2, chunks, 2 * chunks))
    finish_sends(jnp.where(s == 0, 3 * chunks, chunks))


def body(tiles, surface, surface_mask, kappa, remap_weights, remap_columns):
    rows, fields, cells = surface.shape[1:]
    blocks = remap_weights.shape[2]
    chunks = rows // CHUNK
    half = chunks // 2
    block = (rows, fields, cells)
    dma = pltpu.SemaphoreType.DMA
    bf16 = jnp.bfloat16
    return pl.pallas_call(
        functools.partial(kernel, tiles),
        out_shape=jax.ShapeDtypeStruct(surface.shape, F32),
        in_specs=[pl.BlockSpec(memory_space=pltpu.HBM)] * 5,
        out_specs=pl.BlockSpec(memory_space=pltpu.VMEM),
        scratch_shapes=[
            pltpu.VMEM(block, F32),
            pltpu.VMEM((rows, cells), jnp.int32),
            pltpu.VMEM((1, fields), F32),
            pltpu.VMEM((rows, blocks, cells, cells), bf16),
            pltpu.SMEM((blocks, rows), jnp.int32),
            pltpu.VMEM(block, bf16),
            pltpu.VMEM((9 * rows, fields, cells), bf16),
            pltpu.VMEM((rows // 2, fields, cells), bf16),
            pltpu.VMEM((2, SWEEPS, fields, cells), F32),
            pltpu.VMEM((2, SWEEPS, fields, cells), F32),
            pltpu.VMEM((2, SWEEPS, fields, cells), F32),
            dma((4,)),
            dma((WPIECES,)),
            dma((3,)),
            dma((2 * chunks,)),
            dma((3 * chunks,)),
            dma((3 * chunks,)),
            dma((3 * chunks,)),
            dma((3 * chunks,)),
            dma((3 * chunks,)),
            dma((half,)),
            dma((2,)),
            dma((2,)),
        ],
        compiler_params=pltpu.CompilerParams(
            collective_id=0, has_side_effects=True, vmem_limit_bytes=48 * 1024 * 1024
        ),
        name="remap_and_sweep",
    )(surface, surface_mask, kappa, remap_weights, remap_columns[0].T)


def solution(mesh):
    return jax.shard_map(
        functools.partial(body, mesh.shape["tile"]),
        mesh=mesh,
        in_specs=(
            P("section", "tile", None, None),
            P("section", "tile", None),
            P("section", None),
            P("section", "tile", None, None, None),
            P("section", "tile", None),
        ),
        out_specs=P("section", "tile", None, None),
        check_vma=False,
    )
```

time: 102 us -> 41.8 us (0.41)
  the two profiles are of different devices: /device:TPU:6 before, /device:TPU:29 now
where the time goes in v1:
time: 41.8 us; the launch traced here: 41.6 us
  Pallas kernels  37.2 us (89%)
  local copies, waits for them, and re-layouts  4.37 us (10%)
    pallas_call x1, Pallas kernels, body(): pl.pallas_call(functools.partial(kernel, tiles), out_shape=jax.ShapeDtype...  37.2 us
    unnamed x9, local copies, waits for them, and re-layouts  4.37 us

profile of v1, /device:TPU:29, one launch (start us, length us, event | category | flops | bytes accessed | tf_op | source)
XLA Modules:
  0.0 41.6 jit_solution(12836570903490786319)
XLA Ops:
  0.0 0.0 copy-start
  0.0 1.2 %copy-done = f32[1,128,16,128]{3,2,1,0:T(8,128)S(1)} copy-done((f32[1,128,16,128]{3,2,1,0:T(8,128)S(1)}, f32[1,128,16,128]{3,2,1,0:T(8,128)}, u32[]{:S(2)}) %copy-start) | copy-done | bytes 1048600
  1.2 0.0 copy-start.1
  1.2 0.8 %copy-done.1 = s32[1,128,128]{2,1,0:T(8,128)S(1)} copy-done((s32[1,128,128]{2,1,0:T(8,128)S(1)}, s32[1,128,128]{2,1,0:T(8,128)}, u32[]{:S(2)}) %copy-start.1) | copy-done | bytes 65560
  2.1 0.0 copy-start.2
  2.1 0.7 %copy-done.2 = s32[1,128,4]{1,2,0:T(4,128)S(1)} copy-done((s32[1,128,4]{1,2,0:T(4,128)S(1)}, s32[1,128,4]{1,2,0:T(4,128)}, u32[]{:S(2)}) %copy-start.2) | copy-done | bytes 2072
  2.7 0.0 copy-start.3
  2.8 0.7 %copy-done.3 = f32[1,16]{1,0:T(1,128)S(1)} copy-done((f32[1,16]{1,0:T(1,128)S(1)}, f32[1,16]{1,0:T(1,128)}, u32[]{:S(2)}) %copy-start.3) | copy-done | bytes 88
  3.4 37.2 %remap_and_sweep.1 = f32[1,128,16,128]{3,2,1,0:T(8,128)S(1)} custom-call(f32[1,128,16,128]{3,2,1,0:T(8,128)S(1)} %copy-done, s32[1,128,128]{2,1,0:T(8,128)S(1)} %copy-done.1, f32[1,16]{1,0:T(1,128)S(1)} %copy-done.3, bf16[1,128,4,128,128]{4,3,2,1,0:T(8,128)(2,1)} %w_hbm.1, s32[4,128]{1,0:T(4,128)S(1)} %bitcast.3), custom_call_target="tpu_custom_call" | custom-call | tf_op jit(solution)/shard_map/remap_and_sweep/pallas_call | solution.py:359
  40.6 1.0 %copy.7 = f32[1,128,16,128]{3,2,1,0:T(8,128)} copy(f32[1,128,16,128]{3,2,1,0:T(8,128)S(1)} %remap_and_sweep.1) | data formatting | bytes 2097152
Async XLA Ops:
  0.0 1.2 %copy-start = (f32[1,128,16,128]{3,2,1,0:T(8,128)S(1)}, f32[1,128,16,128]{3,2,1,0:T(8,128)}, u32[]{:S(2)}) copy-start(f32[1,128,16,128]{3,2,1,0:T(8,128)} %surf_hbm.1) | copy-start | bytes 3145732
  1.2 0.8 %copy-start.1 = (s32[1,128,128]{2,1,0:T(8,128)S(1)}, s32[1,128,128]{2,1,0:T(8,128)}, u32[]{:S(2)}) copy-start(s32[1,128,128]{2,1,0:T(8,128)} %mask_hbm.1) | copy-start | bytes 196612
  2.1 0.7 %copy-start.2 = (s32[1,128,4]{1,2,0:T(4,128)S(1)}, s32[1,128,4]{1,2,0:T(4,128)}, u32[]{:S(2)}) copy-start(s32[1,128,4]{1,2,0:T(4,128)} %param.9) | copy-start | bytes 6148
  2.7 0.7 %copy-start.3 = (f32[1,16]{1,0:T(1,128)S(1)}, f32[1,16]{1,0:T(1,128)}, u32[]{:S(2)}) copy-start(f32[1,16]{1,0:T(1,128)} %kappa_hbm.1) | copy-start | bytes 196

commit v2 on v1

v2 whole, which is shorter than its diff:
```python
import functools

import jax
import jax.numpy as jnp
from jax import lax
from jax.experimental import pallas as pl
from jax.experimental.pallas import tpu as pltpu
from jax.sharding import PartitionSpec as P

SWEEPS = 4
TIME_STEP = 0.5
ZONAL_RATIO = 0.25

CHUNK = 16
GROUP = 28
WPIECES = 32

NN = (((1,), (0,)), ((), ()))
F32 = jnp.float32


def remote(src, dst, send_sem, recv_sem, where):
    return pltpu.make_async_remote_copy(
        src_ref=src, dst_ref=dst, send_sem=send_sem, recv_sem=recv_sem,
        device_id=where, device_id_type=pl.DeviceIdType.MESH,
    )


def kernel(
    tiles, surf_hbm, mask_hbm, kappa_hbm, w_hbm, cols_hbm, out_hbm,
    surf, mask, kappa, w, cols, place, index, sent, win, relay, edge, near, halo, out,
    surf_sem, w_sem, in_sem, out_sem,
    z_send, z_recv, up_send, down_send, low_recv, high_recv, relay_recv, halo_send, halo_recv,
):
    rows, fields, cells = surf.shape
    blocks = w.shape[1]
    chunks = rows // CHUNK
    half = chunks // 2
    total = rows * tiles
    s = lax.axis_index("section")
    t = lax.axis_index("tile")
    s_up, s_down = lax.rem(s + 1, 4), lax.rem(s + 3, 4)
    has_low, has_high = t > 0, t < tiles - 1

    barrier = pltpu.get_barrier_semaphore()
    for where in ({"section": s_up}, {"section": s_down}):
        pl.semaphore_signal(barrier, inc=1, device_id=where, device_id_type=pl.DeviceIdType.MESH)

    @pl.when(has_low)
    def _():
        pl.semaphore_signal(barrier, inc=1, device_id={"tile": t - 1}, device_id_type=pl.DeviceIdType.MESH)

    @pl.when(has_high)
    def _():
        pl.semaphore_signal(barrier, inc=1, device_id={"tile": t + 1}, device_id_type=pl.DeviceIdType.MESH)

    surf_in = [
        pltpu.make_async_copy(
            surf_hbm.at[0, pl.ds(p * (rows // 4), rows // 4)], surf.at[pl.ds(p * (rows // 4), rows // 4)], surf_sem.at[p]
        )
        for p in range(4)
    ]
    for copy in surf_in:
        copy.start()
    small_in = [
        pltpu.make_async_copy(cols_hbm, cols, in_sem.at[0]),
        pltpu.make_async_copy(mask_hbm.at[0], mask, in_sem.at[1]),
        pltpu.make_async_copy(kappa_hbm, kappa, in_sem.at[2]),
    ]
    for copy in small_in:
        copy.start()
    piece = rows // WPIECES

    def w_in(p):
        part = pl.ds(p * piece, piece)
        return pltpu.make_async_copy(w_hbm.at[0, part], w.at[part], w_sem.at[p])

    def turn(p, _):
        w_in(p).wait()
        for r in range(piece):
            for k in range(blocks):
                w[p * piece + r, k] = w[p * piece + r, k].T
        return 0

    for p in range(4):
        surf_in[p].wait()
        part = pl.ds(p * (rows // 4), rows // 4)
        sent[part] = surf[part].astype(jnp.bfloat16)
    for p in range(WPIECES):
        w_in(p).start()

    small_in[0].wait()
    offset = (1 - t) * rows - jnp.where(s == 0, 3 * rows, 0)
    column = cols[...]
    place[...] = jnp.clip(column - (column // total) * (total - 3 * rows) + offset, 0, 9 * rows - 1)
    place_out = pltpu.make_async_copy(place, index, in_sem.at[3])
    place_out.start()

    pl.semaphore_wait(barrier, 2 + has_low.astype(jnp.int32) + has_high.astype(jnp.int32))

    def at(start, q):
        return win.at[pl.ds(start + q * CHUNK, CHUNK)]

    def mine(q):
        return sent.at[pl.ds(q * CHUNK, CHUNK)]

    def to_low(base, q, n):
        return remote(at(base + rows, q), at(base + 2 * rows, q), down_send, high_recv, {"tile": t - 1})

    def to_high(base, q, n):
        return remote(at(base + rows, q), at(base, q), up_send, low_recv, {"tile": t + 1})

    def spread(base, q, n):
        @pl.when(has_low)
        def _():
            to_low(base, q, n).start()

        @pl.when(has_high)
        def _():
            to_high(base, q, n).start()

    def arrived(base, q, n):
        remote(mine(q), at(base + rows, q), z_send, z_recv.at[n], {"section": s_up}).wait_recv()

    def side(ref, count):
        part = ref.at[pl.ds(0, count)]
        return lambda send, recv, where: remote(part, part, send, recv, where)

    def finish(count):
        @pl.when(has_low)
        def _():
            side(win, count)(up_send, low_recv, {"tile": t - 1}).wait_recv()

        @pl.when(has_high)
        def _():
            side(win, count)(down_send, high_recv, {"tile": t + 1}).wait_recv()

    def finish_sends(count, z_count):
        @pl.when(has_low)
        def _():
            side(win, count)(down_send, high_recv, {"tile": t - 1}).wait_send()

        @pl.when(has_high)
        def _():
            side(win, count)(up_send, low_recv, {"tile": t + 1}).wait_send()

        side(win, z_count)(z_send, low_recv, {"section": s_up}).wait_send()

    @pl.when(s == 0)
    def _():
        for q in range(chunks):
            remote(mine(q), at(rows, q), z_send, z_recv.at[q], {"section": s_up}).start()
            other = (q + half) % chunks
            remote(mine(other), at(rows, other), z_send, z_recv.at[other], {"section": s_down}).start()

        part = WPIECES // (2 * chunks)

        def direct(q, _):
            for src in (0, 2):
                n = src * chunks + q
                arrived(src * 3 * rows, q, n)
                spread(src * 3 * rows, q, n)
                lax.fori_loop((2 * q + src // 2) * part, (2 * q + src // 2 + 1) * part, turn, 0)
            return 0

        lax.fori_loop(0, chunks, direct, 0)

        def relayed(q, _):
            for h in range(2):
                n = chunks + h * half + q
                arrived(3 * rows, h * half + q, n)
                spread(3 * rows, h * half + q, n)
            return 0

        lax.fori_loop(0, half, relayed, 0)
        finish(3 * rows)

    @pl.when((s == 1) | (s == 3))
    def _():
        h = s // 2
        base = (s - 1) * (3 * rows)
        part = WPIECES // (4 * half)
        far = 2
        for q in range(chunks):
            remote(mine(q), at(base + rows, q), z_send, z_recv.at[(s - 1) * chunks + q], {"section": 0}).start()

        def step(q, _):
            own = h * half + q
            held = relay.at[pl.ds(q * CHUNK, CHUNK)]
            arrived(0, own, own)
            remote(at(rows, own), at(rows, own), z_send, z_recv.at[own], {"section": far}).start()
            spread(0, own, own)
            remote(mine(q), held, z_send, relay_recv.at[q], {"section": far}).wait_recv()
            remote(
                held, at(4 * rows, own), z_send, z_recv.at[chunks + own], {"section": 0}
            ).start()
            lax.fori_loop(q * part, (q + 1) * part, turn, 0)
            return 0

        lax.fori_loop(0, half, step, 0)

        def rest(q, _):
            other = (1 - h) * half + q
            arrived(0, other, other)
            spread(0, other, other)
            lax.fori_loop(half * part + q * 3 * part, half * part + (q + 1) * 3 * part, turn, 0)
            return 0

        lax.fori_loop(0, half, rest, 0)
        finish(rows)

    @pl.when(s == 2)
    def _():
        part = WPIECES // half
        for q in range(half):
            held = relay.at[pl.ds(q * CHUNK, CHUNK)]
            remote(mine(q), held, z_send, relay_recv.at[q], {"section": 1}).start()
            remote(mine(half + q), held, z_send, relay_recv.at[q], {"section": 3}).start()

        def step(q, _):
            for n in (q, half + q):
                arrived(0, n, n)
                spread(0, n, n)
            lax.fori_loop(q * part, (q + 1) * part, turn, 0)
            return 0

        lax.fori_loop(0, half, step, 0)
        finish(rows)

    for copy in small_in[1:]:
        copy.wait()
    place_out.wait()

    lane = lax.broadcasted_iota(jnp.int32, (fields, fields), 1)
    sub = lax.broadcasted_iota(jnp.int32, (fields, fields), 0)
    diag = jnp.where(lane == sub, jnp.broadcast_to(kappa[0:1, :], (fields, fields)), 0.0)
    kap = jnp.broadcast_to(jnp.sum(diag, axis=1, keepdims=True), (fields, cells))
    inv = 1.0 / (1.0 + 2.0 * kap + 2.0 * (ZONAL_RATIO * kap))
    a = kap * inv
    b = ZONAL_RATIO * kap * inv

    def forced(r):
        picks, weights = [], []
        for k in range(blocks):
            picks.append(win[index[k, r]])
            weights.append(w[r, k])
        forcing = lax.dot_general(
            jnp.concatenate(picks, axis=1), jnp.concatenate(weights, axis=0), NN, preferred_element_type=F32
        )
        scale = TIME_STEP * mask[pl.ds(r, 1), :].astype(F32)
        return surf[r] + scale * forcing

    def swept(base, low, mid, high):
        zonal = pltpu.roll(mid, 1, 1) + pltpu.roll(mid, cells - 1, 1)
        return base + a * (low + high) + b * zonal

    def advance(state, row):
        levels, bases = state
        levels, bases = [list(x) for x in levels], list(bases)
        bases.append(row * inv)
        levels[0].append(row)
        new = None
        for n in range(SWEEPS):
            if len(levels[n]) < 3:
                return (levels, bases), None
            new = swept(bases[-2 - n], *levels[n][-3:])
            levels[n] = levels[n][-2:]
            if n + 1 < SWEEPS:
                levels[n + 1].append(new)
        return (levels, bases[-SWEEPS - 1:]), new

    low_rows = [forced(r) for r in range(SWEEPS)]
    high_rows = [forced(rows - SWEEPS + r) for r in range(SWEEPS)]
    for r in range(SWEEPS):
        edge[0, r] = low_rows[r]
        edge[1, r] = high_rows[r]
    halo_low = remote(edge.at[0], halo.at[1], halo_send.at[0], halo_recv.at[1], {"tile": t - 1})
    halo_high = remote(edge.at[1], halo.at[0], halo_send.at[1], halo_recv.at[0], {"tile": t + 1})
    pl.when(has_low)(halo_low.start)
    pl.when(has_high)(halo_high.start)

    state = ([[] for _ in range(SWEEPS)], [])
    for r in range(2 * SWEEPS):
        if r < SWEEPS:
            row = low_rows[r]
        else:
            row = forced(r)
            near[0, r - SWEEPS] = row
        state, done = advance(state, row)
        if done is not None:
            out[r - SWEEPS] = done

    def pack(state):
        levels, bases = state
        return tuple(x for level in levels for x in level) + tuple(bases[-SWEEPS:])

    def unpack(flat):
        return [list(flat[2 * n : 2 * n + 2]) for n in range(SWEEPS)], list(flat[2 * SWEEPS :])

    first = 2 * SWEEPS
    count = (rows - 2 * SWEEPS - first) // GROUP - 1

    def put(start, size):
        part = pl.ds(start, size)
        return pltpu.make_async_copy(out.at[part], out_hbm.at[0, part], out_sem)

    def group(g, flat):
        state = unpack(flat)
        for u in range(GROUP):
            r = first + g * GROUP + u
            state, done = advance(state, forced(r))
            out[r - SWEEPS] = done
        put(first - SWEEPS + g * GROUP, GROUP).start()
        return pack(state)

    state = unpack(lax.fori_loop(0, count, group, pack(state)))

    pl.when(has_low)(halo_high.wait_recv)
    pl.when(has_high)(halo_low.wait_recv)

    def end_rows(values, outside, lost):
        values = [jnp.where(lost, 0.0, v) if outside(i) else v for i, v in enumerate(values)]
        bases = [v * inv for v in values]
        level = values
        for n in range(SWEEPS):
            level = [
                jnp.where(lost, 0.0, v) if outside(n + 1 + i) else v
                for i, v in enumerate(
                    swept(bases[n + i], *level[i - 1 : i + 2]) for i in range(1, len(level) - 1)
                )
            ]
        return level

    low_values = [halo[0, r] for r in range(SWEEPS)] + [edge[0, r] for r in range(SWEEPS)]
    low_values += [near[0, r] for r in range(SWEEPS)]
    for r, v in enumerate(end_rows(low_values, lambda i: i < SWEEPS, jnp.logical_not(has_low))):
        out[r] = v
    for r in range(first + count * GROUP, rows):
        if r < rows - SWEEPS:
            row = forced(r)
            if r >= rows - 2 * SWEEPS:
                near[1, r - (rows - 2 * SWEEPS)] = row
        else:
            row = edge[1, r - (rows - SWEEPS)]
        state, done = advance(state, row)
        out[r - SWEEPS] = done

    high_values = [near[1, r] for r in range(SWEEPS)] + [edge[1, r] for r in range(SWEEPS)]
    high_values += [halo[1, r] for r in range(SWEEPS)]
    for r, v in enumerate(end_rows(high_values, lambda i: i >= 2 * SWEEPS, jnp.logical_not(has_high))):
        out[rows - SWEEPS + r] = v

    put(0, SWEEPS).start()
    put(first - SWEEPS + count * GROUP, rows - (first - SWEEPS + count * GROUP)).start()

    pl.when(has_low)(halo_low.wait_send)
    pl.when(has_high)(halo_high.wait_send)

    @pl.when(s == 0)
    def _():
        finish_sends(3 * rows, 2 * rows)

    @pl.when((s == 1) | (s == 3))
    def _():
        finish_sends(rows, 2 * rows)

    @pl.when(s == 2)
    def _():
        finish_sends(rows, rows)

    put(0, rows).wait()

def body(tiles, surface, surface_mask, kappa, remap_weights, remap_columns):
    rows, fields, cells = surface.shape[1:]
    blocks = remap_weights.shape[2]
    chunks = rows // CHUNK
    half = chunks // 2
    block = (rows, fields, cells)
    dma = pltpu.SemaphoreType.DMA
    bf16 = jnp.bfloat16
    return pl.pallas_call(
        functools.partial(kernel, tiles),
        out_shape=jax.ShapeDtypeStruct(surface.shape, F32),
        in_specs=[pl.BlockSpec(memory_space=pltpu.HBM)] * 5,
        out_specs=pl.BlockSpec(memory_space=pl.ANY),
        scratch_shapes=[
            pltpu.VMEM(block, F32),
            pltpu.VMEM((rows, cells), jnp.int32),
            pltpu.VMEM((1, fields), F32),
            pltpu.VMEM((rows, blocks, cells, cells), bf16),
            pltpu.VMEM((blocks, rows), jnp.int32),
            pltpu.VMEM((blocks, rows), jnp.int32),
            pltpu.SMEM((blocks, rows), jnp.int32),
            pltpu.VMEM(block, bf16),
            pltpu.VMEM((9 * rows, fields, cells), bf16),
            pltpu.VMEM((rows // 2, fields, cells), bf16),
            pltpu.VMEM((2, SWEEPS, fields, cells), F32),
            pltpu.VMEM((2, SWEEPS, fields, cells), F32),
            pltpu.VMEM((2, SWEEPS, fields, cells), F32),
            pltpu.VMEM(block, F32),
            dma((4,)),
            dma((WPIECES,)),
            dma((4,)),
            dma(()),
            dma(()),
            dma((3 * chunks,)),
            dma(()),
            dma(()),
            dma(()),
            dma(()),
            dma((half,)),
            dma((2,)),
            dma((2,)),
        ],
        compiler_params=pltpu.CompilerParams(
            collective_id=0, has_side_effects=True, vmem_limit_bytes=60 * 1024 * 1024
        ),
        name="remap_and_sweep",
    )(surface, surface_mask, kappa, remap_weights, remap_columns[0].T)


def solution(mesh):
    return jax.shard_map(
        functools.partial(body, mesh.shape["tile"]),
        mesh=mesh,
        in_specs=(
            P("section", "tile", None, None),
            P("section", "tile", None),
            P("section", None),
            P("section", "tile", None, None, None),
            P("section", "tile", None),
        ),
        out_specs=P("section", "tile", None, None),
        check_vma=False,
    )
```

time: 41.8 us -> 37.9 us (0.907)
  the two profiles are of different devices: /device:TPU:29 before, /device:TPU:6 now
where the time goes in v2:
time: 37.9 us; the launch traced here: 37.8 us
  Pallas kernels  35.5 us (94%)
  local copies, waits for them, and re-layouts  2.26 us (6%)
    pallas_call x1, Pallas kernels, body(): pl.pallas_call(functools.partial(kernel, tiles), out_shape=jax.ShapeDtype...  35.5 us
    unnamed x1, local copies, waits for them, and re-layouts  2.26 us

profile of v2, /device:TPU:6, one launch (start us, length us, event | category | flops | bytes accessed | tf_op | source)
XLA Modules:
  0.0 37.8 jit_solution(10715531545308754767)
XLA Ops:
  0.0 35.5 %remap_and_sweep.1 = f32[1,128,16,128]{3,2,1,0:T(8,128)} custom-call(f32[1,128,16,128]{3,2,1,0:T(8,128)} %surf_hbm.1, s32[1,128,128]{2,1,0:T(8,128)} %mask_hbm.1, f32[1,16]{1,0:T(1,128)} %kappa_hbm.1, bf16[1,128,4,128,128]{4,3,2,1,0:T(8,128)(2,1)} %w_hbm.1, s32[4,128]{1,0:T(4,128)} %bitcast.3), custom_call_target="tpu_custom_call" | custom-call | tf_op jit(solution)/shard_map/remap_and_sweep/pallas_call | solution.py:381
  35.5 2.3 %copy.7 = f32[1,128,16,128]{3,2,1,0:T(8,128)} copy(f32[1,128,16,128]{3,2,1,0:T(8,128)} %remap_and_sweep.1) | data formatting | bytes 2097152

commit v3 on v2

--- a/solution.py
+++ b/solution.py
@@ -413,10 +413,10 @@
             dma((2,)),
         ],
         compiler_params=pltpu.CompilerParams(
-            collective_id=0, has_side_effects=True, vmem_limit_bytes=60 * 1024 * 1024
+            collective_id=0, has_side_effects=True, vmem_limit_bytes=44 * 1024 * 1024
         ),
         name="remap_and_sweep",
-    )(surface, surface_mask, kappa, remap_weights, remap_columns[0].T)
+    )(*[pltpu.with_memory_space_constraint(v, pltpu.HBM) for v in (surface, surface_mask, kappa, remap_weights, remap_columns[0].T)])
 
 
 def solution(mesh):

time: 37.9 us -> 36 us (0.950)
  local copies, waits for them, and re-layouts: 2.26 us -> 0.97 us
  Pallas kernels: 35.5 us -> 34.9 us
    unnamed x1, local copies, waits for them, and re-layouts: 2.26 us -> 0.97 us
    pallas_call x1, Pallas kernels: 35.5 us -> 34.9 us  [body(): pl.pallas_call(functools.partial(kernel, tiles), out_shape=jax.ShapeDtype...]
where the time goes in v3:
time: 36 us; the launch traced here: 35.9 us
  Pallas kernels  34.9 us (97%)
  local copies, waits for them, and re-layouts  0.97 us (3%)
    pallas_call x1, Pallas kernels, body(): pl.pallas_call(functools.partial(kernel, tiles), out_shape=jax.ShapeDtype...  34.9 us
    unnamed x1, local copies, waits for them, and re-layouts  0.97 us

profile of v3, /device:TPU:6, one launch (start us, length us, event | category | flops | bytes accessed | tf_op | source)
XLA Modules:
  0.0 35.9 jit_solution(11602993347906264473)
XLA Ops:
  0.0 34.9 %remap_and_sweep.1 = f32[1,128,16,128]{3,2,1,0:T(8,128)S(1)} custom-call(f32[1,128,16,128]{3,2,1,0:T(8,128)} %surf_hbm.1, s32[1,128,128]{2,1,0:T(8,128)} %mask_hbm.1, f32[1,16]{1,0:T(1,128)} %kappa_hbm.1, bf16[1,128,4,128,128]{4,3,2,1,0:T(8,128)(2,1)} %w_hbm.1, s32[4,128]{1,0:T(4,128)} %bitcast.3), custom_call_target="tpu_custom_call" | custom-call | tf_op jit(solution)/shard_map/remap_and_sweep/pallas_call | solution.py:381
  34.9 1.0 %copy.7 = f32[1,128,16,128]{3,2,1,0:T(8,128)} copy(f32[1,128,16,128]{3,2,1,0:T(8,128)S(1)} %remap_and_sweep.1) | data formatting | bytes 2097152

commit v4 on v3

--- a/solution.py
+++ b/solution.py
@@ -12,7 +12,7 @@
 ZONAL_RATIO = 0.25
 
 CHUNK = 16
-GROUP = 28
+TAIL = 8
 WPIECES = 32
 
 NN = (((1,), (0,)), ((), ()))
@@ -290,30 +290,25 @@
         if done is not None:
             out[r - SWEEPS] = done
 
-    def pack(state):
-        levels, bases = state
-        return tuple(x for level in levels for x in level) + tuple(bases[-SWEEPS:])
-
-    def unpack(flat):
-        return [list(flat[2 * n : 2 * n + 2]) for n in range(SWEEPS)], list(flat[2 * SWEEPS :])
-
-    first = 2 * SWEEPS
-    count = (rows - 2 * SWEEPS - first) // GROUP - 1
-
     def put(start, size):
         part = pl.ds(start, size)
         return pltpu.make_async_copy(out.at[part], out_hbm.at[0, part], out_sem)
 
-    def group(g, flat):
-        state = unpack(flat)
-        for u in range(GROUP):
-            r = first + g * GROUP + u
-            state, done = advance(state, forced(r))
-            out[r - SWEEPS] = done
-        put(first - SWEEPS + g * GROUP, GROUP).start()
-        return pack(state)
-
-    state = unpack(lax.fori_loop(0, count, group, pack(state)))
+    def interior(state, first, last):
+        for r in range(first, last):
+            if r < rows - SWEEPS:
+                row = forced(r)
+                if r >= rows - 2 * SWEEPS:
+                    near[1, r - (rows - 2 * SWEEPS)] = row
+            else:
+                row = edge[1, r - (rows - SWEEPS)]
+            state, done = advance(state, row)
+            if done is not None:
+                out[r - SWEEPS] = done
+        return state
+
+    state = interior(state, 2 * SWEEPS, rows - TAIL)
+    put(SWEEPS, rows - TAIL - 2 * SWEEPS).start()
 
     pl.when(has_low)(halo_high.wait_recv)
     pl.when(has_high)(halo_low.wait_recv)
@@ -335,23 +330,14 @@
     low_values += [near[0, r] for r in range(SWEEPS)]
     for r, v in enumerate(end_rows(low_values, lambda i: i < SWEEPS, jnp.logical_not(has_low))):
         out[r] = v
-    for r in range(first + count * GROUP, rows):
-        if r < rows - SWEEPS:
-            row = forced(r)
-            if r >= rows - 2 * SWEEPS:
-                near[1, r - (rows - 2 * SWEEPS)] = row
-        else:
-            row = edge[1, r - (rows - SWEEPS)]
-        state, done = advance(state, row)
-        out[r - SWEEPS] = done
-
+    interior(state, rows - TAIL, rows)
     high_values = [near[1, r] for r in range(SWEEPS)] + [edge[1, r] for r in range(SWEEPS)]
     high_values += [halo[1, r] for r in range(SWEEPS)]
     for r, v in enumerate(end_rows(high_values, lambda i: i >= 2 * SWEEPS, jnp.logical_not(has_high))):
         out[rows - SWEEPS + r] = v
 
     put(0, SWEEPS).start()
-    put(first - SWEEPS + count * GROUP, rows - (first - SWEEPS + count * GROUP)).start()
+    put(rows - TAIL - SWEEPS, TAIL + SWEEPS).start()
 
     pl.when(has_low)(halo_low.wait_send)
     pl.when(has_high)(halo_high.wait_send)

time: 36 us -> 35.4 us (0.983)
  Pallas kernels: 34.9 us -> 34.3 us
    pallas_call x1, Pallas kernels: 34.9 us -> 34.3 us  [body(): pl.pallas_call(functools.partial(kernel, tiles), out_shape=jax.ShapeDtype...]
where the time goes in v4:
time: 35.4 us; the launch traced here: 35.3 us
  Pallas kernels  34.3 us (97%)
  local copies, waits for them, and re-layouts  0.97 us (3%)
    pallas_call x1, Pallas kernels, body(): pl.pallas_call(functools.partial(kernel, tiles), out_shape=jax.ShapeDtype...  34.3 us
    unnamed x1, local copies, waits for them, and re-layouts  0.97 us

profile of v4, /device:TPU:6, one launch (start us, length us, event | category | flops | bytes accessed | tf_op | source)
XLA Modules:
  0.0 35.3 jit_solution(16535961713152291994)
XLA Ops:
  0.0 34.3 %remap_and_sweep.1 = f32[1,128,16,128]{3,2,1,0:T(8,128)S(1)} custom-call(f32[1,128,16,128]{3,2,1,0:T(8,128)} %surf_hbm.1, s32[1,128,128]{2,1,0:T(8,128)} %mask_hbm.1, f32[1,16]{1,0:T(1,128)} %kappa_hbm.1, bf16[1,128,4,128,128]{4,3,2,1,0:T(8,128)(2,1)} %w_hbm.1, s32[4,128]{1,0:T(4,128)} %bitcast.3), custom_call_target="tpu_custom_call" | custom-call | tf_op jit(solution)/shard_map/remap_and_sweep/pallas_call | solution.py:367
  34.3 1.0 %copy.7 = f32[1,128,16,128]{3,2,1,0:T(8,128)} copy(f32[1,128,16,128]{3,2,1,0:T(8,128)S(1)} %remap_and_sweep.1) | data formatting | bytes 2097152
